TPU v7x, 128 devices: a whole 4x4x4 slice. The times are simulated.
128 devices in a mesh: ctx: 32 (over z, y_lo, x), head: 4 (over y_hi, core).
Axes of the slice: x: 4, y: 4 (y_hi: 2, y_lo: 2; y = y_hi * 2 + y_lo), z: 4, core: 2. Of those that a mesh axis runs over, the one named last changes fastest.
Arguments:
- events: bfloat16 [24576, 1024], P('ctx', 'head'), may hold values from -3 to 3
- norm_gain: float32 [1024], replicated, may hold values from 0.5 to 1.5
- w_uvqk: bfloat16 [1024, 4, 1024], P(None, None, 'head'), may hold values from -4 to 4
- w_out: bfloat16 [1024, 1024], P('head'), may hold values from -0.1875 to 0.1875
- lengths: int32 [8], replicated, may hold values from 1 to 13824, 24576 in all
Outputs:
- mixed: bfloat16 [24576, 1024], P('ctx', 'head')
Inputs may be any that keep to these rules, and one draw needn't show every extreme that they name: The lengths sum to 24576; the longest is exactly 13824.
All inputs are finite; a program needn't handle non-finite values.
Results may differ from a plain program's by a relative error of at most 0.0062.
Values may be sent and summed in bfloat16 or wider, within the bound.
No kernel may reach another device: no remote copies, remote signals or barrier semaphores. Data moves between devices by JAX's collectives and lax.ppermute only.
A program may use at most 128 MiB of HBM per device.

v0:
```python
import jax
import jax.numpy as jnp
from jax import lax
from jax.sharding import PartitionSpec as P

D = 1024
HDIM = 128


def attend(totals, key_block, value_block, offset, queries, query_pos, query_seg, seq_ends):
    count = key_block.shape[0]
    key_pos = offset + jnp.arange(count, dtype=jnp.int32)
    key_seg = jnp.sum((key_pos[:, None] >= seq_ends[None, :]).astype(jnp.int32), axis=1)
    score_scale = key_block.shape[-1] ** (-0.5)
    scores = (
        jnp.einsum("qhd,khd->hqk", queries, key_block, preferred_element_type=jnp.float32)
        * score_scale
    )
    allowed = (
        (query_seg[:, None] == key_seg[None, :])
        & (key_pos[None, :] <= query_pos[:, None])
        & (key_pos[None, :] >= 0)
    )
    weights = jnp.where(allowed[None], jax.nn.silu(scores), 0.0).astype(jnp.bfloat16)
    return totals + jnp.einsum(
        "hqk,khd->qhd", weights, value_block, preferred_element_type=jnp.float32
    )


def shards(events, norm_gain, w_uvqk, w_out, lengths):
    epsilon = 1e-05
    row_count = events.shape[0]
    gathered = lax.all_gather(events, "head", axis=1, tiled=True)
    xfloat = gathered.astype(jnp.float32)
    row_mean = jnp.mean(xfloat, axis=-1, keepdims=True)
    centered = xfloat - row_mean
    row_var = jnp.mean(centered * centered, axis=-1, keepdims=True)
    normed = (centered * lax.rsqrt(row_var + epsilon) * norm_gain).astype(jnp.bfloat16)
    local_cols = w_uvqk.shape[2]
    heads_here = local_cols // HDIM
    projected = jax.nn.silu(
        jnp.dot(
            normed,
            w_uvqk.reshape(w_uvqk.shape[0], 4 * local_cols),
            preferred_element_type=jnp.float32,
        )
    ).astype(jnp.bfloat16)
    projected = projected.reshape(row_count, 4, heads_here, HDIM)
    gate_rows = projected[:, 0]
    value_rows = projected[:, 1]
    queries = projected[:, 2]
    key_rows = projected[:, 3]
    seq_ends = jnp.cumsum(lengths)
    seq_starts = seq_ends - lengths
    seq_index = jnp.arange(lengths.shape[0], dtype=jnp.int32)
    my_first = lax.axis_index("ctx") * row_count
    query_pos = my_first + jnp.arange(row_count, dtype=jnp.int32)
    query_seg = jnp.sum((query_pos[:, None] >= seq_ends[None, :]).astype(jnp.int32), axis=1)
    empty = jnp.zeros((row_count, heads_here, HDIM), jnp.float32)
    history_start = jnp.sum(jnp.where(query_seg[0] == seq_index, seq_starts, 0))
    last_row = my_first + row_count - 1
    key_all = lax.all_gather(key_rows, "ctx", axis=0, tiled=True)
    value_all = lax.all_gather(value_rows, "ctx", axis=0, tiled=True)
    block_rows = min(key_all.shape[0], row_count)
    turns = key_all.shape[0] // block_rows

    def inner(turn_index, running):
        lower = turn_index * block_rows
        key_block = lax.dynamic_slice_in_dim(key_all, lower, block_rows, 0)
        value_block = lax.dynamic_slice_in_dim(value_all, lower, block_rows, 0)
        needed = (lower + block_rows > history_start) & (lower <= last_row)

        def take_block(current):
            return attend(
                current, key_block, value_block, lower, queries, query_pos, query_seg, seq_ends
            )

        def skip_block(current):
            return current

        return lax.cond(needed, take_block, skip_block, running)

    attended = lax.fori_loop(0, turns, inner, empty)
    local_squares = jnp.sum(attended * attended, axis=(1, 2))
    squares = lax.psum(local_squares, "head")
    inverse_rms = lax.rsqrt(squares / D + epsilon)
    gated = (
        (attended * inverse_rms[:, None, None] * gate_rows.astype(jnp.float32))
        .astype(jnp.bfloat16)
        .reshape(row_count, local_cols)
    )
    partial_out = jnp.dot(gated, w_out, preferred_element_type=jnp.float32)
    shared = lax.psum_scatter(partial_out, "head", scatter_dimension=1, tiled=True)
    return (events.astype(jnp.float32) + shared).astype(jnp.bfloat16)


def solution(mesh):
    in_specs = (P("ctx", "head"), P(), P(None, None, "head"), P("head", None), P())
    out_specs = P("ctx", "head")
    return jax.shard_map(shards, mesh=mesh, in_specs=in_specs, out_specs=out_specs, check_vma=False)
```

profile of v0, /device:TPU:1, one launch (start us, length us, event | category | flops | bytes accessed | tf_op | source)
XLA Modules:
  0.0 572.1 jit_solution(18329584764954480928)
XLA Ops:
  6.5 0.7 all-gather.6.cloned.1.call-update
  7.3 2.1 copy.28
  9.4 27.1 %all-gather.6.cloned.1.call-done = bf16[768,1024]{1,0:T(8,128)(2,1)} async-done(((bf16[768,256]{1,0:T(8,128)(2,1)}), bf16[768,1024]{1,0:T(8,128)(2,1)}) %all-gather.6.cloned.1.call-update) | async-done | bytes 1572880 | tf_op jit(solution)/shard_map/all_gather | solution.py:33
  36.5 1.8 convert_reduce_fusion.1
  38.3 2.0 fusion.27
  40.3 3.4 multiply_convert_fusion
  43.7 2.8 reshape.139
  46.5 1.1 fusion.39
  47.6 0.8 copy.24
  48.5 0.8 copy.26
  49.4 0.0 reduce-scatter.2.cloned.1.call-start
  49.4 0.2 reduce-window.8
  49.6 0.1 convert_reduce_fusion.2
  49.7 0.5 slice.15
  50.2 1.3 fusion.38
  51.6 0.4 copy.27
  52.0 0.1 copy.30
  52.1 152.2 %all-gather.8.cloned.1.call-done = bf16[24576,1,2,128]{3,0,2,1:T(8,128)(2,1)} async-done(((bf16[768,1,2,128]{3,0,2,1:T(8,128)(2,1)}), bf16[24576,1,2,128]{3,0,2,1:T(8,128)(2,1)}) %all-gather.8.cloned.1.call-update) | async-done | bytes 12582928 | tf_op jit(solution)/shard_map/all_gather | solution.py:62
  204.2 175.0 %all-gather.10.cloned.1.call-done = bf16[24576,1,2,128]{3,0,2,1:T(8,128)(2,1)} async-done(((bf16[768,1,2,128]{3,0,2,1:T(8,128)(2,1)}), bf16[24576,1,2,128]{3,0,2,1:T(8,128)(2,1)}) %all-gather.10.cloned.1.call-update) | async-done | bytes 12582928 | tf_op jit(solution)/shard_map/all_gather | solution.py:63
  379.3 0.1 broadcast_in_dim.40
  379.3 28.9 %while.17 = (s32[]{:T(128)}, f32[768,2,128]{2,0,1:T(8,128)S(1)}, s32[]{:T(128)}, s32[]{:T(128)}, s32[768]{0:T(1024)S(1)}, /*index=5*/s32[8]{0:T(128)S(1)}, bf16[...) while((s32[]{:T(128)}, f32[768,2,128]{2,0,1:T(8,128)S(1)}, ...), condition=%wide.region_9.10_spmd.clone, body=%wide.region_5.9_spmd.clone.sunk | while | flops 614813952 | bytes 3965765 | solution.py:83
  380.0 4.9 conditional.3
  380.1 0.1 convert_reduce_fusion
  380.2 0.8 and_and_fusion
  381.0 3.9 fusion.14
  408.2 0.2 multiply_reduce_fusion
  408.4 0.3 copy.21
  408.7 25.6 %psum.7 = f32[768]{0:T(1024)S(1)} all-reduce(f32[768]{0:T(1024)S(1)} %multiply_reduce_fusion), channel_id=1, replica_groups=mesh['ctx'=32,'head'=4] {'head'}, use_global_device_ids=true, to_apply=%region_11.12 | all-reduce | flops 768 | bytes 6144 | tf_op jit(solution)/shard_map/psum | solution.py:85
  434.3 0.1 fusion.37
  434.4 2.3 fusion.40
  436.7 126.9 %reduce-scatter.2.cloned.1.call-done = f32[768,256]{1,0:T(8,128)} async-done(((f32[768,1024]{1,0:T(8,128)}), f32[768,256]{1,0:T(8,128)}) %reduce-scatter.2.cloned.1.call-update) | async-done | bytes 786448 | tf_op jit(solution)/shard_map/reduce_scatter | solution.py:93
  563.6 2.0 add_convert_fusion
  (85 shorter events, 0.8 us)
Async XLA Ops:
  6.5 427.8 %copy-start = (bf16[256,1024]{1,0:T(8,128)(2,1)S(1)}, bf16[256,1024]{1,0:T(8,128)(2,1)}, u32[]{:S(2)}) copy-start(bf16[256,1024]{1,0:T(8,128)(2,1)} %param.12) | copy-start | bytes 1572868
  6.5 30.0 %all-gather.6.cloned.1.call-start = ((), (), s32[]{:S(2)}) async-start(), calls=%async_computation.1 | async-start | bytes 1966080 | tf_op jit(solution)/shard_map/all_gather | solution.py:33
  7.3 197.0 %all-gather.8.cloned.1.call-start = ((), (), s32[]{:S(2)}) async-start(), calls=%async_computation.3 | async-start | bytes 12976128 | tf_op jit(solution)/shard_map/all_gather | solution.py:62
  7.3 33.0 %copy-start.4 = (f32[1024]{0:T(1024)S(1)}, f32[1024]{0:T(1024)}, u32[]{:S(2)}) copy-start(f32[1024]{0:T(1024)} %param.10) | copy-start | bytes 12292
  36.5 3.8 copy-start.1
  46.5 2.9 copy-start.3
  48.5 330.8 %all-gather.10.cloned.1.call-start = ((), (), s32[]{:S(2)}) async-start(), calls=%async_computation.4 | async-start | bytes 12976128 | tf_op jit(solution)/shard_map/all_gather | solution.py:63
  49.4 514.2 %reduce-scatter.2.cloned.1.call-start = ((), (), s32[]{:S(2)}) async-start(), calls=%async_computation.2 | async-start | bytes 3932160 | tf_op jit(solution)/shard_map/reduce_scatter | solution.py:93
  434.4 129.2 %copy-start.2 = (bf16[768,256]{1,0:T(8,128)(2,1)S(1)}, bf16[768,256]{1,0:T(8,128)(2,1)}, u32[]{:S(2)}) copy-start(bf16[768,256]{1,0:T(8,128)(2,1)} %param.9) | copy-start | bytes 1179652
Sparse Core Ops, SparseCore 0:
  9.0 27.4 all-gather.5
  48.6 155.6 all-gather.7
  205.9 173.3 all-gather.9
  436.8 126.7 reduce-scatter.1
where the time goes:
time: 573 us; the launch traced here: 572 us
  waiting for transfers between devices  482 us (84%)
  blocking collectives  25.6 us (4%)
  loops' own time  23.9 us (4%)
  between operations  13.3 us (2%)
  matrix products  9.58 us (2%)
  local copies, waits for them, and re-layouts  9.07 us (2%)
  other arithmetic  8.59 us (1%)
    all_gather x1, waiting for transfers between devices, shards(): value_all = lax.all_gather(value_rows, 'ctx', axis=0, tiled=True)  175 us
    all_gather x1, waiting for transfers between devices, shards(): key_all = lax.all_gather(key_rows, 'ctx', axis=0, tiled=True)  152 us
    reduce_scatter x1, waiting for transfers between devices, shards(): lax.psum_scatter(partial_out, 'head', scatter_dimension=1, tiled=True)  127 us
    all_gather x1, waiting for transfers between devices, shards(): gathered = lax.all_gather(events, 'head', axis=1, tiled=True)  27.1 us
    psum x1, blocking collectives, shards(): squares = lax.psum(local_squares, 'head')  25.6 us
    another operation x1, loops' own time, shards(): attended = lax.fori_loop(0, turns, inner, empty)  23.3 us
  transfers between devices with their start and end apart: 4, of which 4 were waited for; matrix products, arithmetic and copies ran while one was open for 1% of the time, Pallas kernels for 0%

commit v1 on v0

--- a/solution.py
+++ b/solution.py
@@ -59,8 +59,11 @@
     empty = jnp.zeros((row_count, heads_here, HDIM), jnp.float32)
     history_start = jnp.sum(jnp.where(query_seg[0] == seq_index, seq_starts, 0))
     last_row = my_first + row_count - 1
-    key_all = lax.all_gather(key_rows, "ctx", axis=0, tiled=True)
-    value_all = lax.all_gather(value_rows, "ctx", axis=0, tiled=True)
+    key_all, value_all = jnp.split(
+        lax.all_gather(jnp.concatenate([key_rows, value_rows], axis=1), "ctx", axis=0, tiled=True),
+        [key_rows.shape[1]],
+        axis=1,
+    )
     block_rows = min(key_all.shape[0], row_count)
     turns = key_all.shape[0] // block_rows
 

time: 573 us -> 518 us (0.904)
  waiting for transfers between devices: 482 us -> 430 us
  blocking collectives: 25.6 us -> 7.37 us
  local copies, waits for them, and re-layouts: 9.07 us -> 24.5 us
    all_gather x2 -> x1, waiting for transfers between devices: 327 us -> 274 us  [shards(): lax.all_gather(jnp.concatenate([key_rows, value_rows], axis=1), 'ctx', ax...]
    psum x1, blocking collectives: 25.6 us -> 7.37 us  [shards(): squares = lax.psum(local_squares, 'head')]
    split x0 -> x1, local copies, waits for them, and re-layouts: none -> 16.9 us  [shards(): jnp.split(lax.all_gather(jnp.concatenate([key_rows, value_rows], axis=1),...]
  transfers between devices with their start and end apart: 4 -> 3, of which waited for: 4 -> 3; matrix products, arithmetic and copies ran while one was open for 1% -> 1% of each run, Pallas kernels for 0% -> 0%
where the time goes in v1:
time: 518 us; the launch traced here: 517 us
  waiting for transfers between devices  430 us (83%)
  local copies, waits for them, and re-layouts  24.5 us (5%)
  loops' own time  23.5 us (5%)
  between operations  13.3 us (3%)
  matrix products  9.55 us (2%)
  other arithmetic  9.54 us (2%)
  blocking collectives  7.37 us (1%)
    all_gather x1, waiting for transfers between devices, shards(): lax.all_gather(jnp.concatenate([key_rows, value_rows], axis=1), 'ctx', ax...  274 us
    reduce_scatter x1, waiting for transfers between devices, shards(): lax.psum_scatter(partial_out, 'head', scatter_dimension=1, tiled=True)  128 us
    all_gather x1, waiting for transfers between devices, shards(): gathered = lax.all_gather(events, 'head', axis=1, tiled=True)  27.1 us
    another operation x1, loops' own time, shards(): attended = lax.fori_loop(0, turns, inner, empty)  23 us
    split x1, local copies, waits for them, and re-layouts, shards(): jnp.split(lax.all_gather(jnp.concatenate([key_rows, value_rows], axis=1),...  16.9 us
  transfers between devices with their start and end apart: 3, of which 3 were waited for; matrix products, arithmetic and copies ran while one was open for 1% of the time, Pallas kernels for 0%

profile of v1, /device:TPU:1, one launch (start us, length us, event | category | flops | bytes accessed | tf_op | source)
XLA Modules:
  0.0 517.4 jit_solution(5259224613004817962)
XLA Ops:
  6.5 0.7 all-gather.3.cloned.1.call-update
  7.3 2.1 copy.28
  9.4 27.1 %all-gather.3.cloned.1.call-done = bf16[768,1024]{1,0:T(8,128)(2,1)} async-done(((bf16[768,256]{1,0:T(8,128)(2,1)}), bf16[768,1024]{1,0:T(8,128)(2,1)}) %all-gather.3.cloned.1.call-update) | async-done | bytes 1572880 | tf_op jit(solution)/shard_map/all_gather | solution.py:33
  36.5 1.8 convert_reduce_fusion.1
  38.3 2.0 fusion.27
  40.3 3.4 multiply_convert_fusion
  43.7 2.8 reshape.139
  46.5 1.1 fusion.40
  47.6 0.1 copy_bitcast_fusion.1
  47.7 1.0 pad_maximum_fusion
  48.8 0.0 reduce-scatter.2.cloned.1.call-start
  48.8 0.2 reduce-window.8
  49.0 0.1 convert_reduce_fusion.2
  49.1 0.5 slice.15
  49.7 1.3 fusion.38
  51.0 0.1 copy.32
  51.0 0.4 copy.27
  51.5 274.0 %all-gather.5.cloned.1.call-done = bf16[24576,4,128]{2,0,1:T(8,128)(2,1)} async-done(((bf16[768,4,128]{2,0,1:T(8,128)(2,1)}), bf16[24576,4,128]{2,0,1:T(8,128)(2,1)}) %all-gather.5.cloned.1.call-update) | async-done | bytes 25165840 | tf_op jit(solution)/shard_map/all_gather | solution.py:63
  325.5 16.9 %fusion.39 = (bf16[24576,2,128]{2,0,1:T(8,128)(2,1)}, bf16[24576,2,128]{2,0,1:T(8,128)(2,1)}) fusion(bf16[24576,4,128]{2,0,1:T(8,128)(2,1)} %all-gather.5.cloned.1.call-done), kind=kLoop, calls=%fused_computation.50 | loop fusion | bytes 50331648 | tf_op jit(solution)/shard_map/split | solution.py:62
  342.4 0.1 broadcast_in_dim.40
  342.5 28.4 %while.17 = (s32[]{:T(128)}, f32[768,2,128]{2,0,1:T(8,128)S(1)}, s32[]{:T(128)}, s32[]{:T(128)}, s32[768]{0:T(1024)S(1)}, /*index=5*/s32[8]{0:T(128)S(1)}, bf16[...) while((s32[]{:T(128)}, f32[768,2,128]{2,0,1:T(8,128)S(1)}, ...), condition=%wide.region_9.10_spmd.clone, body=%wide.region_5.9_spmd.clone.sunk | while | flops 614813952 | bytes 3965765 | solution.py:86
  343.2 4.9 conditional.3
  343.2 0.1 convert_reduce_fusion
  343.3 0.8 and_and_fusion
  344.2 3.9 fusion.14
  370.9 0.3 copy.21
  371.2 0.2 multiply_reduce_fusion
  371.3 7.4 %psum.7 = f32[768]{0:T(1024)S(1)} all-reduce(f32[768]{0:T(1024)S(1)} %multiply_reduce_fusion), channel_id=1, replica_groups=mesh['ctx'=32,'head'=4] {'head'}, use_global_device_ids=true, to_apply=%region_11.12 | all-reduce | flops 768 | bytes 6144 | tf_op jit(solution)/shard_map/psum | solution.py:88
  378.7 0.1 fusion.37
  378.8 2.3 fusion.41
  381.1 127.7 %reduce-scatter.2.cloned.1.call-done = f32[768,256]{1,0:T(8,128)} async-done(((f32[768,1024]{1,0:T(8,128)}), f32[768,256]{1,0:T(8,128)}) %reduce-scatter.2.cloned.1.call-update) | async-done | bytes 786448 | tf_op jit(solution)/shard_map/reduce_scatter | solution.py:96
  508.9 2.0 add_convert_fusion
  (83 shorter events, 0.6 us)
Async XLA Ops:
  6.5 372.3 %copy-start = (bf16[256,1024]{1,0:T(8,128)(2,1)S(1)}, bf16[256,1024]{1,0:T(8,128)(2,1)}, u32[]{:S(2)}) copy-start(bf16[256,1024]{1,0:T(8,128)(2,1)} %param.12) | copy-start | bytes 1572868
  6.5 30.0 %all-gather.3.cloned.1.call-start = ((), (), s32[]{:S(2)}) async-start(), calls=%async_computation.1 | async-start | bytes 1966080 | tf_op jit(solution)/shard_map/all_gather | solution.py:33
  7.3 318.2 %all-gather.5.cloned.1.call-start = ((), (), s32[]{:S(2)}) async-start(), calls=%async_computation.2 | async-start | bytes 25952256 | tf_op jit(solution)/shard_map/all_gather | solution.py:63
  7.3 33.0 %copy-start.4 = (f32[1024]{0:T(1024)S(1)}, f32[1024]{0:T(1024)}, u32[]{:S(2)}) copy-start(f32[1024]{0:T(1024)} %param.10) | copy-start | bytes 12292
  36.5 3.8 copy-start.1
  46.5 2.3 copy-start.3
  48.8 460.1 %reduce-scatter.2.cloned.1.call-start = ((), (), s32[]{:S(2)}) async-start(), calls=%async_computation.3 | async-start | bytes 3932160 | tf_op jit(solution)/shard_map/reduce_scatter | solution.py:96
  378.8 130.0 %copy-start.2 = (bf16[768,256]{1,0:T(8,128)(2,1)S(1)}, bf16[768,256]{1,0:T(8,128)(2,1)}, u32[]{:S(2)}) copy-start(bf16[768,256]{1,0:T(8,128)(2,1)} %param.9) | copy-start | bytes 1179652
Sparse Core Ops, SparseCore 0:
  9.0 27.4 all-gather.2
  48.9 276.5 all-gather.4
  381.3 127.5 reduce-scatter.1
